TPU v7x, 256 devices: a whole 4x4x8 slice. The times are simulated.
256 devices in a mesh: wide: 32 (over y, x, core), narrow: 8 (over z).
Axes of the slice: x: 4, y: 4, z: 8, core: 2. Of those that a mesh axis runs over, the one named last changes fastest.
Arguments:
- three_centre: bfloat16 [32, 1024, 4096], P('narrow', 'wide'), may hold values from -6 to 6
- go_blocks: bfloat16 [64, 64, 64], replicated, may hold values from -0.75 to 0.75
- gv_blocks: bfloat16 [64, 64, 64], replicated, may hold values from -0.125 to 0.125
- go_index: int32 [32, 32], P('narrow'), may hold values from 0 to 63
- gv_index: int32 [32, 32], P('narrow'), may hold values from 0 to 63
- source_mask: int32 [32, 32], P('narrow'), may hold values 0 or 1
Outputs:
- chi: float32 [1024, 1024], P('wide', 'narrow')
All inputs are finite; a program needn't handle non-finite values. No bound on the sum of `source_mask` on one device may be relied on, other than what follows from the above.
Results may differ from a plain program's by a relative error of at most 0.004.
Values may be sent and summed in bfloat16 or wider, within the bound.
No kernel may reach another device: no remote copies, remote signals or barrier semaphores. Data moves between devices by JAX's collectives and lax.ppermute only.
A program may use at most 192 MiB of HBM per device.

v0:
```python
import jax
import jax.numpy as jnp
from jax import lax
from jax.sharding import PartitionSpec as P


def local(three_centre, go_blocks, gv_blocks, go_index, gv_index, source_mask):
    local_pairs, aux_local, pair_width = three_centre.shape
    block = go_blocks.shape[1]
    go_chosen = go_blocks[go_index]
    gv_chosen = gv_blocks[gv_index] * source_mask.astype(jnp.bfloat16)[:, :, None, None]
    piece = lax.all_gather(three_centre, "narrow", axis=0, tiled=True)
    number_sources = piece.shape[0]
    sources = piece.reshape(number_sources, aux_local, block, block)
    results = []
    for target in range(local_pairs):
        first_product = jnp.einsum(
            "cma,cpmn->cpan", go_chosen[target], sources, preferred_element_type=jnp.float32
        ).astype(jnp.bfloat16)
        results.append(
            jnp.einsum(
                "cpan,cnd->pad",
                first_product,
                gv_chosen[target],
                preferred_element_type=jnp.float32,
            )
        )
    summed = jnp.stack(results)
    image = summed.reshape(local_pairs, aux_local, pair_width).astype(jnp.bfloat16)
    norm_scale = 1.0 / jnp.sqrt(jnp.float32(local_pairs * lax.axis_size("narrow") * pair_width))
    partial_chi = jnp.einsum(
        "kpe,kqe->pq",
        image,
        lax.all_gather(three_centre, "wide", axis=1, tiled=True),
        preferred_element_type=jnp.float32,
    )
    result = lax.psum_scatter(partial_chi, "narrow", scatter_dimension=1, tiled=True)
    return result * norm_scale


def solution(mesh):
    placed = (
        P("narrow", "wide", None),
        P(),
        P(),
        P("narrow", None),
        P("narrow", None),
        P("narrow", None),
    )
    return jax.shard_map(
        local, mesh=mesh, in_specs=placed, out_specs=P("wide", "narrow"), check_vma=False
    )
```

profile of v0, /device:TPU:12, one launch (start us, length us, event | category | flops | bytes accessed | tf_op | source)
XLA Modules:
  0.0 286.2 jit_solution(9310431331818708807)
XLA Ops:
  6.5 0.7 all-gather.3.cloned.1.call-update
  7.3 0.7 all-gather.5.cloned.1.call-update
  8.1 0.7 compare_select_fusion
  8.7 0.1 reshape.28
  8.8 0.7 convert_element_type.30
  9.5 0.7 compare_select_fusion.1
  10.2 0.1 reshape.20
  10.3 1.0 gather_fusion.1
  11.3 3.4 %gather_fusion = bf16[128,64,64]{2,1,0:T(8,128)(2,1)} fusion(bf16[64,64,64]{2,1,0:T(8,128)(2,1)} %param.7, s32[1024]{0:T(1024)S(1)} %pad_clamp_fusion.1), kind=kCustom, calls=%fused_computation | custom fusion | bytes 2097664 | tf_op jit(solution)/shard_map/gather | solution.py:10
  14.7 1.5 broadcast_multiply_fusion
  16.2 90.0 %all-gather.3.cloned.1.call-done = bf16[32,32,4096]{2,1,0:T(8,128)(2,1)} async-done(((bf16[4,32,4096]{2,1,0:T(8,128)(2,1)}), bf16[32,32,4096]{2,1,0:T(8,128)(2,1)}) %all-gather.3.cloned.1.call-update) | async-done | bytes 8388624 | tf_op jit(solution)/shard_map/all_gather | solution.py:12
  106.2 23.6 %reshape.17 = bf16[32,32,64,64]{3,2,1,0:T(8,128)(2,1)} reshape(bf16[32,32,4096]{2,1,0:T(8,128)(2,1)} %all-gather.3.cloned.1.call-done) | data formatting | bytes 16777216 | tf_op jit(solution)/shard_map/reshape | solution.py:14
  129.8 10.7 %fusion.63 = bf16[32,64,64]{2,1,0:T(8,128)(2,1)S(1)} fusion(bf16[32,32,64,64]{3,2,1,0:T(8,128)(2,1)} %reshape.17, bf16[4,32,64,64]{3,2,1,0:T(8,128)(2,1)S(1)} %copy-done.2, bf16[128,64,64]{2,1,0:T(8,128)(2,1)} %gather_fusion), kind=kOutput, calls=%fused_computation.29 | convolution fusion | flops 1078067200 | bytes 18087936 | tf_op jit(solution)/shard_map/cpan,cnd->pad/dot_general | solution.py:21
  140.6 0.5 stack.15
  141.0 10.6 %fusion.58 = bf16[32,64,64]{2,1,0:T(8,128)(2,1)S(1)} fusion(bf16[32,32,64,64]{3,2,1,0:T(8,128)(2,1)} %reshape.17, bf16[4,32,64,64]{3,2,1,0:T(8,128)(2,1)S(1)} %copy-done.2, bf16[128,64,64]{2,1,0:T(8,128)(2,1)} %gather_fusion), kind=kOutput, calls=%fused_computation.28 | convolution fusion | flops 1078067200 | bytes 18087936 | tf_op jit(solution)/shard_map/cpan,cnd->pad/dot_general | solution.py:21
  151.6 1.2 stack.16
  152.8 12.7 %fusion.53 = bf16[32,64,64]{2,1,0:T(8,128)(2,1)S(1)} fusion(bf16[32,32,64,64]{3,2,1,0:T(8,128)(2,1)} %reshape.17, bf16[4,32,64,64]{3,2,1,0:T(8,128)(2,1)S(1)} %copy-done.2, bf16[128,64,64]{2,1,0:T(8,128)(2,1)} %gather_fusion), kind=kOutput, calls=%fused_computation.27 | convolution fusion | flops 1078067200 | bytes 18087936 | tf_op jit(solution)/shard_map/cpan,cnd->pad/dot_general | solution.py:21
  165.5 1.2 stack.17
  166.7 11.7 %fusion.48 = bf16[32,64,64]{2,1,0:T(8,128)(2,1)} fusion(bf16[32,32,64,64]{3,2,1,0:T(8,128)(2,1)} %reshape.17, bf16[4,32,64,64]{3,2,1,0:T(8,128)(2,1)S(1)} %copy-done.2, bf16[128,64,64]{2,1,0:T(8,128)(2,1)} %gather_fusion), kind=kOutput, calls=%fused_computation.26 | convolution fusion | flops 1078067200 | bytes 18087936 | tf_op jit(solution)/shard_map/cpan,cnd->pad/dot_general | solution.py:21
  178.4 1.6 stack.18
  180.0 44.6 %all-gather.5.cloned.1.call-done = bf16[4,1024,4096]{2,1,0:T(8,128)(2,1)} async-done(((bf16[4,32,4096]{2,1,0:T(8,128)(2,1)}), bf16[4,1024,4096]{2,1,0:T(8,128)(2,1)}) %all-gather.5.cloned.1.call-update) | async-done | bytes 33554448 | tf_op jit(solution)/shard_map/all_gather | solution.py:34
  224.6 16.0 %convolution_bitcast_fusion = f32[32,1024]{1,0:T(8,128)} fusion(bf16[4,1024,4096]{2,1,0:T(8,128)(2,1)} %all-gather.5.cloned.1.call-done, bf16[1,32,4096]{2,1,0:T(8,128)(2,1)S(1)} %stack.18, bf16[1,32,4096]{2,1,0:T(8,128)(2,1)} %stack.17, bf16[1,32,4096]{2,1,0:T(8,128)(2,1)} %stack.16, bf16[1,32,4096]{2,1,0:T(8,128)(2,1)S(1)} %stack.15), kind=kOutput, calls=%fused_computation.30 | convolution fusion | flops 1075314688 | bytes 34734080 | tf_op jit(solution)/shard_map/kpe,kqe->pq/dot_general | solution.py:31
  240.6 37.7 %reduce-scatter.2.cloned.1.call-done = f32[32,128]{1,0:T(8,128)} async-done(((f32[32,1024]{1,0:T(8,128)}), f32[32,128]{1,0:T(8,128)}) %reduce-scatter.2.cloned.1.call-update) | async-done | bytes 16400 | tf_op jit(solution)/shard_map/reduce_scatter | solution.py:37
  278.4 1.3 broadcast_multiply_fusion.1
  (12 shorter events, 0.1 us)
Async XLA Ops:
  6.5 3.8 %copy-start = (bf16[64,64,64]{2,1,0:T(8,128)(2,1)S(1)}, bf16[64,64,64]{2,1,0:T(8,128)(2,1)}, u32[]{:S(2)}) copy-start(bf16[64,64,64]{2,1,0:T(8,128)(2,1)} %param.8) | copy-start | bytes 1572868
  6.5 99.6 %all-gather.3.cloned.1.call-start = ((), (), s32[]{:S(2)}) async-start(), calls=%async_computation.1 | async-start | bytes 9437184 | tf_op jit(solution)/shard_map/all_gather | solution.py:12
  7.3 217.3 %all-gather.5.cloned.1.call-start = ((), (), s32[]{:S(2)}) async-start(), calls=%async_computation.2 | async-start | bytes 34603008 | tf_op jit(solution)/shard_map/all_gather | solution.py:34
  8.0 270.4 %reduce-scatter.2.cloned.1.call-start = ((), (), s32[]{:S(2)}) async-start(), calls=%async_computation.3 | async-start | bytes 147456 | tf_op jit(solution)/shard_map/reduce_scatter | solution.py:37
  16.2 113.6 %copy-start.2 = (bf16[4,32,64,64]{3,2,1,0:T(8,128)(2,1)S(1)}, bf16[4,32,64,64]{3,2,1,0:T(8,128)(2,1)}, u32[]{:S(2)}) copy-start(bf16[4,32,64,64]{3,2,1,0:T(8,128)(2,1)} %broadcast_multiply_fusion) | copy-start | bytes 3145732
  178.4 101.3 %copy-start.1 = (bf16[64,64,64]{2,1,0:T(8,128)(2,1)S(1)}, bf16[64,64,64]{2,1,0:T(8,128)(2,1)}, u32[]{:S(2)}) copy-start(bf16[64,64,64]{2,1,0:T(8,128)(2,1)} %param.8) | copy-start | bytes 1572868
Sparse Core Ops, SparseCore 0:
  9.1 96.9 all-gather.2
  108.8 115.7 all-gather.4
  240.7 37.5 reduce-scatter.1
where the time goes:
time: 287 us; the launch traced here: 286 us
  waiting for transfers between devices  174 us (61%)
  matrix products  61.8 us (22%)
  local copies, waits for them, and re-layouts  32.6 us (11%)
  between operations  13.2 us (5%)
  other arithmetic  4.92 us (2%)
    all_gather x1, waiting for transfers between devices, local(): piece = lax.all_gather(three_centre, 'narrow', axis=0, tiled=True)  90 us
    dot_general x4, matrix products, local(): jnp.einsum('cpan,cnd->pad', first_product, gv_chosen[target], preferred_e...  45.7 us
    all_gather x1, waiting for transfers between devices, local(): lax.all_gather(three_centre, 'wide', axis=1, tiled=True)  44.6 us
    reduce_scatter x1, waiting for transfers between devices, local(): lax.psum_scatter(partial_chi, 'narrow', scatter_dimension=1, tiled=True)  37.7 us
    reshape x1, local copies, waits for them, and re-layouts, local(): sources = piece.reshape(number_sources, aux_local, block, block)  23.6 us
    dot_general x1, matrix products, local(): jnp.einsum('kpe,kqe->pq', image, lax.all_gather(three_centre, 'wide', axi...  16 us
  transfers between devices with their start and end apart: 3, of which 3 were waited for; matrix products, arithmetic and copies ran while one was open for 29% of the time, Pallas kernels for 0%

commit v1 on v0

--- a/solution.py
+++ b/solution.py
@@ -9,7 +9,9 @@
     block = go_blocks.shape[1]
     go_chosen = go_blocks[go_index]
     gv_chosen = gv_blocks[gv_index] * source_mask.astype(jnp.bfloat16)[:, :, None, None]
-    piece = lax.all_gather(three_centre, "narrow", axis=0, tiled=True)
+    piece = jnp.concatenate(
+        lax.all_to_all(jnp.stack([three_centre] * lax.axis_size("narrow")), "narrow", 0, 0), axis=0
+    )
     number_sources = piece.shape[0]
     sources = piece.reshape(number_sources, aux_local, block, block)
     results = []

time: 287 us -> 337 us (1.17)
  waiting for transfers between devices: 174 us -> 214 us
  starting transfers between devices: 0.08 us -> 8.54 us
  local copies, waits for them, and re-layouts: 32.6 us -> 38 us
    all_to_all x0 -> x1, waiting for transfers between devices: none -> 180 us  [local(): lax.all_to_all(jnp.stack([three_centre] * lax.axis_size('narrow')), 'narr...]
    all_gather x1 -> x0, waiting for transfers between devices: 90 us -> none  [local(): piece = lax.all_gather(three_centre, 'narrow', axis=0, tiled=True)]
    all_gather x1, waiting for transfers between devices: 44.6 us -> 0.02 us  [local(): lax.all_gather(three_centre, 'wide', axis=1, tiled=True)]
    another operation x0 -> x2, local copies, waits for them, and re-layouts: none -> 29.1 us  [the longest x1 23.6 us: local(): sources = piece.reshape(number_sources, aux_local, block, block)]
    reshape x1 -> x0, local copies, waits for them, and re-layouts: 23.6 us -> none  [local(): sources = piece.reshape(number_sources, aux_local, block, block)]
    all_to_all x0 -> x1, starting transfers between devices: none -> 8.47 us  [local(): lax.all_to_all(jnp.stack([three_centre] * lax.axis_size('narrow')), 'narr...]
    reduce_scatter x1, waiting for transfers between devices: 37.7 us -> 32.9 us  [local(): lax.psum_scatter(partial_chi, 'narrow', scatter_dimension=1, tiled=True)]
  transfers between devices with their start and end apart: 3 -> 3, of which waited for: 3 -> 2; matrix products, arithmetic and copies ran while one was open for 29% -> 25% of each run, Pallas kernels for 0% -> 0%
where the time goes in v1:
time: 337 us; the launch traced here: 336 us
  waiting for transfers between devices  214 us (64%)
  matrix products  59 us (18%)
  local copies, waits for them, and re-layouts  38 us (11%)
  between operations  13.5 us (4%)
  starting transfers between devices  8.54 us (3%)
    all_to_all x1, waiting for transfers between devices, local(): lax.all_to_all(jnp.stack([three_centre] * lax.axis_size('narrow')), 'narr...  180 us
    dot_general x4, matrix products, local(): jnp.einsum('cpan,cnd->pad', first_product, gv_chosen[target], preferred_e...  43 us
    reduce_scatter x1, waiting for transfers between devices, local(): lax.psum_scatter(partial_chi, 'narrow', scatter_dimension=1, tiled=True)  32.9 us
    another operation x1, local copies, waits for them, and re-layouts, local(): sources = piece.reshape(number_sources, aux_local, block, block)  23.6 us
    dot_general x1, matrix products, local(): jnp.einsum('kpe,kqe->pq', image, lax.all_gather(three_centre, 'wide', axi...  16 us
    all_to_all x1, starting transfers between devices, local(): lax.all_to_all(jnp.stack([three_centre] * lax.axis_size('narrow')), 'narr...  8.47 us
  transfers between devices with their start and end apart: 3, of which 2 were waited for; matrix products, arithmetic and copies ran while one was open for 25% of the time, Pallas kernels for 0%

profile of v1, /device:TPU:12, one launch (start us, length us, event | category | flops | bytes accessed | tf_op | source)
XLA Modules:
  0.0 336.0 jit_solution(11022660631016363681)
XLA Ops:
  6.5 0.0 all-gather.2.cloned.1.call-start
  6.6 0.7 all-gather.2.cloned.1.call-update
  7.3 5.5 %stack.12 = bf16[8,4,32,4096]{3,2,1,0:T(8,128)(2,1)} broadcast(bf16[4,32,4096]{2,1,0:T(8,128)(2,1)} %param.6), dimensions={1,2,3} | broadcast | bytes 9437184 | tf_op jit(solution)/shard_map/stack | solution.py:13
  12.8 8.5 %all-to-all-start = ((bf16[8,4,32,4096]{3,2,1,0:T(8,128)(2,1)}), bf16[8,4,32,4096]{3,2,1,0:T(8,128)(2,1)}, u32[]{:S(2)}, u32[]{:S(2)}) async-start(bf16[8,4,32,4096]{3,2,1,0:T(8,128)(2,1)} %stack.12), calls=%async_computation | async-start | bytes 16777216 | tf_op jit(solution)/shard_map/all_to_all | solution.py:13
  21.2 0.0 reduce-scatter.2.cloned.1.call-start
  21.3 0.1 reshape.26
  21.4 0.1 reshape.18
  21.5 1.0 gather_fusion.1
  22.5 3.4 %gather_fusion = bf16[128,64,64]{2,1,0:T(8,128)(2,1)} fusion(bf16[64,64,64]{2,1,0:T(8,128)(2,1)} %param.7, s32[1024]{0:T(1024)S(1)} %pad_clamp_fusion.1), kind=kCustom, calls=%fused_computation | custom fusion | bytes 2097664 | tf_op jit(solution)/shard_map/gather | solution.py:10
  25.9 1.5 broadcast_multiply_fusion
  27.4 180.4 %all-to-all-done = bf16[8,4,32,4096]{3,2,1,0:T(8,128)(2,1)} async-done(((bf16[8,4,32,4096]{3,2,1,0:T(8,128)(2,1)}), bf16[8,4,32,4096]{3,2,1,0:T(8,128)(2,1)}, u32[]{:S(2)}, u32[]{:S(2)}) %all-to-all-start) | async-done | bytes 8388640 | tf_op jit(solution)/shard_map/all_to_all | solution.py:13
  207.8 23.6 %reshape_reshape.3 = bf16[32,32,64,64]{3,2,1,0:T(8,128)(2,1)} reshape(bf16[8,4,32,4096]{3,2,1,0:T(8,128)(2,1)} %all-to-all-done) | data formatting | bytes 16777216 | tf_op jit(solution)/shard_map/reshape;reshape | solution.py:16
  231.4 10.6 %fusion.63 = bf16[32,64,64]{2,1,0:T(8,128)(2,1)S(1)} fusion(bf16[32,32,64,64]{3,2,1,0:T(8,128)(2,1)} %reshape_reshape.3, bf16[4,32,64,64]{3,2,1,0:T(8,128)(2,1)S(1)} %copy-done.2, bf16[128,64,64]{2,1,0:T(8,128)(2,1)} %gather_fusion), kind=kOutput, calls=%fused_computation.29 | convolution fusion | flops 1078067200 | bytes 18087936 | tf_op jit(solution)/shard_map/cpan,cnd->pad/dot_general | solution.py:23
  242.0 0.5 stack.13
  242.5 10.6 %fusion.58 = bf16[32,64,64]{2,1,0:T(8,128)(2,1)S(1)} fusion(bf16[32,32,64,64]{3,2,1,0:T(8,128)(2,1)} %reshape_reshape.3, bf16[4,32,64,64]{3,2,1,0:T(8,128)(2,1)S(1)} %copy-done.2, bf16[128,64,64]{2,1,0:T(8,128)(2,1)} %gather_fusion), kind=kOutput, calls=%fused_computation.28 | convolution fusion | flops 1078067200 | bytes 18087936 | tf_op jit(solution)/shard_map/cpan,cnd->pad/dot_general | solution.py:23
  253.1 1.2 stack.28
  254.2 10.6 %fusion.53 = bf16[32,64,64]{2,1,0:T(8,128)(2,1)S(1)} fusion(bf16[32,32,64,64]{3,2,1,0:T(8,128)(2,1)} %reshape_reshape.3, bf16[4,32,64,64]{3,2,1,0:T(8,128)(2,1)S(1)} %copy-done.2, bf16[128,64,64]{2,1,0:T(8,128)(2,1)} %gather_fusion), kind=kOutput, calls=%fused_computation.27 | convolution fusion | flops 1078067200 | bytes 18087936 | tf_op jit(solution)/shard_map/cpan,cnd->pad/dot_general | solution.py:23
  264.8 1.2 stack.29
  266.0 11.3 %fusion.48 = bf16[32,64,64]{2,1,0:T(8,128)(2,1)} fusion(bf16[32,32,64,64]{3,2,1,0:T(8,128)(2,1)} %reshape_reshape.3, bf16[4,32,64,64]{3,2,1,0:T(8,128)(2,1)S(1)} %copy-done.2, bf16[128,64,64]{2,1,0:T(8,128)(2,1)} %gather_fusion), kind=kOutput, calls=%fused_computation.26 | convolution fusion | flops 1078067200 | bytes 18087936 | tf_op jit(solution)/shard_map/cpan,cnd->pad/dot_general | solution.py:23
  277.3 1.6 stack.30
  278.9 0.0 all-gather.2.cloned.1.call-done
  278.9 16.0 %convolution_bitcast_fusion = f32[32,1024]{1,0:T(8,128)} fusion(bf16[4,1024,4096]{2,1,0:T(8,128)(2,1)} %all-gather.2.cloned.1.call-done, bf16[1,32,4096]{2,1,0:T(8,128)(2,1)S(1)} %stack.30, bf16[1,32,4096]{2,1,0:T(8,128)(2,1)} %stack.29, bf16[1,32,4096]{2,1,0:T(8,128)(2,1)} %stack.28, bf16[1,32,4096]{2,1,0:T(8,128)(2,1)S(1)} %stack.13), kind=kOutput, calls=%fused_computation.30 | convolution fusion | flops 1075314688 | bytes 34734080 | tf_op jit(solution)/shard_map/kpe,kqe->pq/dot_general | solution.py:33
  294.9 32.9 %reduce-scatter.2.cloned.1.call-done = f32[32,128]{1,0:T(8,128)} async-done(((f32[32,1024]{1,0:T(8,128)}), f32[32,128]{1,0:T(8,128)}) %reduce-scatter.2.cloned.1.call-update) | async-done | bytes 16400 | tf_op jit(solution)/shard_map/reduce_scatter | solution.py:39
  327.9 1.3 broadcast_multiply_fusion.1
  (18 shorter events, 0.1 us)
Async XLA Ops:
  6.5 15.0 %copy-start = (bf16[64,64,64]{2,1,0:T(8,128)(2,1)S(1)}, bf16[64,64,64]{2,1,0:T(8,128)(2,1)}, u32[]{:S(2)}) copy-start(bf16[64,64,64]{2,1,0:T(8,128)(2,1)} %param.8) | copy-start | bytes 1572868
  6.5 14.7 %copy-start.4 = (s32[4,32]{1,0:T(4,128)S(1)}, s32[4,32]{1,0:T(4,128)}, u32[]{:S(2)}) copy-start(s32[4,32]{1,0:T(4,128)} %param.10) | copy-start | bytes 1540
  6.5 14.8 %copy-start.3 = (s32[4,32]{1,0:T(4,128)S(1)}, s32[4,32]{1,0:T(4,128)}, u32[]{:S(2)}) copy-start(s32[4,32]{1,0:T(4,128)} %param.11) | copy-start | bytes 1540
  6.5 14.8 %copy-start.5 = (s32[4,32]{1,0:T(4,128)S(1)}, s32[4,32]{1,0:T(4,128)}, u32[]{:S(2)}) copy-start(s32[4,32]{1,0:T(4,128)} %param.9) | copy-start | bytes 1540
  6.5 272.3 %all-gather.2.cloned.1.call-start = ((), (), s32[]{:S(2)}) async-start(), calls=%async_computation.2 | async-start | bytes 34603008 | tf_op jit(solution)/shard_map/all_gather | solution.py:36
  12.8 195.1 %all-to-all-start = ((bf16[8,4,32,4096]{3,2,1,0:T(8,128)(2,1)}), bf16[8,4,32,4096]{3,2,1,0:T(8,128)(2,1)}, u32[]{:S(2)}, u32[]{:S(2)}) async-start(bf16[8,4,32,4096]{3,2,1,0:T(8,128)(2,1)} %stack.12), calls=%async_computation | async-start | bytes 16777216 | tf_op jit(solution)/shard_map/all_to_all | solution.py:13
  21.2 306.6 %reduce-scatter.2.cloned.1.call-start = ((), (), s32[]{:S(2)}) async-start(), calls=%async_computation.3 | async-start | bytes 147456 | tf_op jit(solution)/shard_map/reduce_scatter | solution.py:39
  27.4 204.0 %copy-start.2 = (bf16[4,32,64,64]{3,2,1,0:T(8,128)(2,1)S(1)}, bf16[4,32,64,64]{3,2,1,0:T(8,128)(2,1)}, u32[]{:S(2)}) copy-start(bf16[4,32,64,64]{3,2,1,0:T(8,128)(2,1)} %broadcast_multiply_fusion) | copy-start | bytes 3145732
  277.3 51.9 %copy-start.1 = (bf16[64,64,64]{2,1,0:T(8,128)(2,1)S(1)}, bf16[64,64,64]{2,1,0:T(8,128)(2,1)}, u32[]{:S(2)}) copy-start(bf16[64,64,64]{2,1,0:T(8,128)(2,1)} %param.8) | copy-start | bytes 1572868
Sparse Core Ops, SparseCore 0:
  10.0 120.0 all-gather.1
  295.1 32.7 reduce-scatter.1
